TPU v7x, 256 devices: a whole 4x4x8 slice. The times are simulated.
256 devices in a mesh: img: 16 (over z, core), txt: 16 (over x, y).
Axes of the slice: x: 4, y: 4, z: 8, core: 2. Of those that a mesh axis runs over, the one named last changes fastest.
Arguments:
- teacher_img: bfloat16 [16384, 1280], P('img'), may hold values from -40 to 40
- teacher_txt: bfloat16 [16384, 1280], P('txt'), may hold values from -40 to 40
- student_img: bfloat16 [16384, 512], P('img'), may hold values from -40 to 40
- student_txt: bfloat16 [16384, 512], P('txt'), may hold values from -40 to 40
Outputs:
- loss: float32 [], replicated
- grad_img: float32 [16384, 512], P(('img', 'txt'))
- grad_txt: float32 [16384, 512], P(('txt', 'img'))
All inputs are finite; a program needn't handle non-finite values.
Results may differ from a plain program's by a relative error of at most 0.0033.
Values sent between devices are 32-bit elements; how exact they have to be, the bound alone decides.
No kernel may reach another device: no remote copies, remote signals or barrier semaphores. Data moves between devices by JAX's collectives and lax.ppermute only.
A program may use at most 64 MiB of HBM per device.

v0:
```python
import math
import jax
import jax.numpy as jnp
from jax import lax
from jax.sharding import Mesh
from jax.sharding import PartitionSpec as P

IMG = ("img_0", "img_1")
TXT = ("txt_0", "txt_1")
IMG_TXT = ("img_0", "img_1", "txt_0", "txt_1")
TXT_IMG = ("txt_0", "txt_1", "img_0", "img_1")


def from_everyone(shard, axis):
    copies = jnp.broadcast_to(shard, (lax.axis_size(axis), *shard.shape))
    return lax.all_to_all(copies, axis, split_axis=0, concat_axis=0, tiled=True)


def collected_together(shard, axis):
    leaves = jax.tree.leaves(shard)
    order = sorted(range(len(leaves)), key=lambda k: -leaves[k].size)
    width = (1, *leaves[order[0]].shape)[-1]
    lines = [
        jnp.pad(leaves[k].reshape(-1), (0, -leaves[k].size % width)).reshape(-1, width)
        for k in order
    ]
    both, at, found = (from_everyone(jnp.concatenate(lines), axis), 0, {})
    for k, line in zip(order, lines):
        piece = both[:, at : at + len(line)].reshape(len(both), -1)
        found[k] = piece[:, : leaves[k].size].reshape(-1, *leaves[k].shape)
        at += len(line)
    numbers = iter(range(len(leaves)))
    return jax.tree.map(lambda _: found[next(numbers)], shard)


def combined_pairwise(pieces, combine):
    while len(jax.tree.leaves(pieces)[0]) > 1:
        pieces = jax.vmap(combine)(
            *(jax.tree.map(lambda part: part[side::2], pieces) for side in (0, 1))
        )
    return jax.tree.map(lambda part: part[0], pieces)


def joined_all(shard, axis, combine):
    pieces = collected_together(shard, axis)
    return combined_pairwise(pieces, combine)


def over_axes(shard, axes):
    for axis in axes:
        shard = lax.psum(shard, axis)
    return shard


def split_up(shard, dim, size):
    dims = shard.shape
    parts = shard.reshape(*dims[:dim], size, dims[dim] // size, *dims[dim + 1 :])
    return jnp.moveaxis(parts, dim, 0)


def sum_by_chip(shard, chips, core, dim):
    sizes = (lax.axis_size(chips), lax.axis_size(core))
    parts = split_up(shard, dim, sizes[0] * sizes[1])
    inside = parts.shape[1:]
    parts = parts.reshape(*sizes, *inside).swapaxes(0, 1).reshape(-1, *inside)
    parts = lax.psum_scatter(parts, core, scatter_dimension=0, tiled=True)
    return lax.psum_scatter(parts, chips, scatter_dimension=0, tiled=True)[0]


def summed_on_arrival(shard, axis, dim):
    size = lax.axis_size(axis)
    parts = lax.all_to_all(split_up(shard, dim, size), axis, 0, 0, tiled=True)
    return jnp.sum(parts, axis=0)


def join_pair(peak_one, mass_one, peak_two, mass_two):
    highest = jnp.maximum(peak_one, peak_two)
    return (
        highest,
        mass_one * jnp.exp(peak_one - highest) + mass_two * jnp.exp(peak_two - highest),
    )


def combine_masses(first, second):
    teach_peak, teach_mass = join_pair(first[0], first[1], second[0], second[1])
    learn_peak, learn_mass = join_pair(first[2], first[3], second[2], second[3])
    return (teach_peak, teach_mass, learn_peak, learn_mass)


def local_masses(teacher, student, along):
    teach_peak = jnp.max(teacher, axis=along)
    learn_peak = jnp.max(student, axis=along)
    teach_mass = jnp.sum(jnp.exp(teacher - jnp.expand_dims(teach_peak, along)), axis=along)
    learn_mass = jnp.sum(jnp.exp(student - jnp.expand_dims(learn_peak, along)), axis=along)
    return (teach_peak, teach_mass, learn_peak, learn_mass)


def body(teacher_img, teacher_txt, student_img, student_txt):
    scale_teach = 3.0 / math.sqrt(teacher_img.shape[1])
    scale_learn = 3.0 / math.sqrt(student_img.shape[1])
    rows = teacher_img.shape[0]
    cols = teacher_txt.shape[0]
    img_count = lax.axis_size(IMG)
    txt_count = lax.axis_size(TXT)
    teacher = scale_teach * jnp.einsum(
        "id,jd->ij", teacher_img, teacher_txt, preferred_element_type=jnp.float32
    )
    student = scale_learn * jnp.einsum(
        "id,jd->ij", student_img, student_txt, preferred_element_type=jnp.float32
    )
    row_tpeak, row_tmass, row_lpeak, row_lmass = joined_all(
        local_masses(teacher, student, 1), TXT, combine_masses
    )
    col_tpeak, col_tmass, col_lpeak, col_lmass = joined_all(
        local_masses(teacher, student, 0), IMG, combine_masses
    )
    row_teach = row_tpeak + jnp.log(row_tmass)
    row_learn = row_lpeak + jnp.log(row_lmass)
    col_teach = col_tpeak + jnp.log(col_tmass)
    col_learn = col_lpeak + jnp.log(col_lmass)
    p_row = jnp.exp(teacher - row_teach[:, None])
    q_row = jnp.exp(student - row_learn[:, None])
    p_col = jnp.exp(teacher - col_teach[None, :])
    q_col = jnp.exp(student - col_learn[None, :])
    gap = teacher - student
    row_part = (jnp.sum(p_row * gap) + jnp.sum(row_learn - row_teach) / txt_count) / (
        rows * img_count
    )
    col_part = (jnp.sum(p_col * gap) + jnp.sum(col_learn - col_teach) / img_count) / (
        cols * txt_count
    )
    delta = (8.0 * (q_row - p_row + q_col - p_col)).astype(jnp.bfloat16)
    loss = 0.5 * over_axes(row_part + col_part, IMG_TXT)
    picked = delta
    grad_txt = sum_by_chip(
        scale_learn
        * jnp.einsum("ij,id->jd", picked, student_img, preferred_element_type=jnp.float32),
        "img_0",
        "img_1",
        0,
    )
    picked = delta
    grad_img = summed_on_arrival(
        scale_learn * jnp.dot(picked, student_txt, preferred_element_type=jnp.float32), TXT, 0
    )
    return (loss, grad_img, grad_txt)


def solution(mesh):
    torus = Mesh(mesh.devices.reshape(8, 2, 4, 4), ("img_0", "img_1", "txt_0", "txt_1"))
    in_specs = (P(IMG, None), P(TXT, None), P(IMG, None), P(TXT, None))
    out_specs = (P(), P(IMG_TXT, None), P(TXT_IMG, None))
    return jax.shard_map(body, mesh=torus, in_specs=in_specs, out_specs=out_specs, check_vma=False)
```

profile of v0, /device:TPU:0, one launch (start us, length us, event | category | flops | bytes accessed | tf_op | source)
XLA Modules:
  0.0 146.1 jit_solution(15397041045933169511)
XLA Ops:
  7.2 0.0 copy-start
  7.2 1.7 %copy-done = bf16[1024,1280]{1,0:T(8,128)(2,1)S(1)} copy-done((bf16[1024,1280]{1,0:T(8,128)(2,1)S(1)}, bf16[1024,1280]{1,0:T(8,128)(2,1)}, u32[]{:S(2)}) %copy-start) | copy-done | bytes 2621464
  8.9 4.8 %multiply_reduce_fusion.4 = (f32[1024]{0:T(1024)S(1)}, f32[1024]{0:T(1024)S(1)}, f32[1024,1024]{1,0:T(8,128)S(1)}) fusion(bf16[1024,1280]{1,0:T(8,128)(2,1)S(1)} %copy-done, bf16[1024,1280]{1,0:T(8,128)(2,1)} %param.5), kind=kOutput, calls=%fused_computation.12 | convolution fusion | flops 2687498240 | bytes 9445376 | tf_op jit(solution)/shard_map/id,jd->ij/dot_general | solution.py:105
  13.7 1.4 multiply_reduce_fusion.2
  15.1 0.6 copy-done.1
  15.7 1.6 %exponential_reduce_fusion.1 = (f32[1024]{0:T(1024)S(1)}, f32[1024]{0:T(1024)S(1)}) fusion(f32[1024,1024]{1,0:T(8,128)S(1)} %get-tuple-element.50, f32[1024]{0:T(1024)S(1)} %get-tuple-element.7, f32[1024]{0:T(1024)S(1)} %get-tuple-element.8), kind=kLoop, calls=%fused_computation.4 | loop fusion | flops 5240832 | bytes 4210688 | tf_op jit(solution)/shard_map/reduce_sum | solution.py:93
  17.3 1.6 %exponential_reduce_fusion = (f32[1024]{0:T(1024)S(1)}, f32[1024]{0:T(1024)S(1)}) fusion(f32[1024,1024]{1,0:T(8,128)S(1)} %get-tuple-element.49, f32[1024]{0:T(1024)S(1)} %get-tuple-element.11, f32[1024]{0:T(1024)S(1)} %get-tuple-element.12), kind=kLoop, calls=%fused_computation.3 | loop fusion | flops 5240832 | bytes 4210688 | tf_op jit(solution)/shard_map/reduce_sum | solution.py:94
  18.9 0.8 broadcast_in_dim.4
  19.6 5.3 %all-to-all-start = ((f32[16,4,1024]{2,1,0:T(4,128)}), f32[16,4,1024]{2,1,0:T(4,128)S(1)}, u32[]{:S(2)}, u32[]{:S(2)}) async-start(f32[16,4,1024]{2,1,0:T(4,128)} %broadcast_in_dim.4), calls=%async_computation | async-start | bytes 524288 | tf_op jit(solution)/shard_map/all_to_all | solution.py:16
  25.0 8.5 %all-to-all-done = f32[16,4,1024]{2,1,0:T(4,128)S(1)} async-done(((f32[16,4,1024]{2,1,0:T(4,128)}), f32[16,4,1024]{2,1,0:T(4,128)S(1)}, u32[]{:S(2)}, u32[]{:S(2)}) %all-to-all-start) | async-done | bytes 262176 | tf_op jit(solution)/shard_map/all_to_all | solution.py:16
  33.4 0.8 broadcast_in_dim.5
  34.2 8.6 %all-to-all-start.1 = ((f32[16,4,1024]{2,1,0:T(4,128)}), f32[16,4,1024]{2,1,0:T(4,128)S(1)}, u32[]{:S(2)}, u32[]{:S(2)}) async-start(f32[16,4,1024]{2,1,0:T(4,128)} %broadcast_in_dim.5), calls=%async_computation.1 | async-start | bytes 524288 | tf_op jit(solution)/shard_map/all_to_all | solution.py:16
  42.8 0.2 reduce-scatter.3.cloned.1.call-start
  43.0 0.2 fusion.8
  44.1 9.9 %all-to-all-done.1 = f32[16,4,1024]{2,1,0:T(4,128)S(1)} async-done(((f32[16,4,1024]{2,1,0:T(4,128)}), f32[16,4,1024]{2,1,0:T(4,128)S(1)}, u32[]{:S(2)}, u32[]{:S(2)}) %all-to-all-start.1) | async-done | bytes 262176 | tf_op jit(solution)/shard_map/all_to_all | solution.py:16
  54.0 0.2 fusion.9
  55.0 0.7 subtract_reduce_fusion
  55.6 9.1 %multiply_reduce_fusion = (f32[]{:T(128)}, f32[]{:T(128)}, bf16[1024,1024]{1,0:T(8,128)(2,1)S(1)}) fusion(f32[1024,1024]{1,0:T(8,128)} %copy-done.2, f32[1024,1024]{1,0:T(8,128)} %copy-done.1, f32[1024]{0:T(1024)S(1)} %bitcast.50, f32[1024]{0:T(1024)S(1)} %bitcast.47, f32[1024]{0:T(1024)S(1)} %bitcast.49, f32[1024]{0:T(1024)S(1)} %bitcast.45), kind=kLoop, calls=%fused_computation.1 | loop fusion | flops 16777214 | bytes 10502152 | tf_op jit(solution)/shard_map/reduce_sum | solution.py:129
  64.7 1.3 convolution_multiply_fusion
  66.0 1.6 %copy.21 = f32[2,8,64,512]{3,2,1,0:T(8,128)} copy(f32[2,8,64,512]{3,2,0,1:T(8,128)S(1)} %bitcast.44) | data formatting | bytes 4194304 | tf_op jit(solution)/shard_map/transpose | solution.py:65
  67.6 0.0 reduce-scatter.3.cloned.1.call-update
  67.6 0.0 reduce-scatter.5.cloned.1.call-start
  67.7 9.4 %reduce-scatter.3.cloned.1.call-done = f32[8,64,512]{2,1,0:T(8,128)} async-done(((f32[16,64,512]{2,1,0:T(8,128)}), f32[8,64,512]{2,1,0:T(8,128)}) %reduce-scatter.3.cloned.1.call-update) | async-done | bytes 1048592 | tf_op jit(solution)/shard_map/reduce_scatter | solution.py:66
  77.1 0.0 reduce-scatter.5.cloned.1.call-update
  77.1 4.5 %convolution_multiply_fusion.1 = f32[1024,512]{1,0:T(8,128)} fusion(bf16[1024,1024]{1,0:T(8,128)(2,1)} %copy-done.3, bf16[1024,512]{1,0:T(8,128)(2,1)} %param.7), kind=kOutput, calls=%fused_computation.15 | convolution fusion | flops 1074266112 | bytes 5242880 | tf_op jit(solution)/shard_map/dot_general | solution.py:144
  81.6 6.9 %all-to-all-start.2 = ((f32[16,64,512]{2,1,0:T(8,128)}), f32[16,64,512]{2,1,0:T(8,128)}, u32[]{:S(2)}, u32[]{:S(2)}) async-start(f32[16,64,512]{2,1,0:T(8,128)} %bitcast.43), calls=%async_computation.2 | async-start | bytes 4194304 | tf_op jit(solution)/shard_map/all_to_all | solution.py:72
  88.5 0.6 subtract_reduce_fusion.1
  91.6 18.0 %psum.28 = f32[]{:T(128)} all-reduce(f32[]{:T(128)S(6)} %add.127), channel_id=1, replica_groups=mesh['img_0'=8,'img_1'=2,'txt_0'=4,'txt_1'=4] {'img_0'}, use_global_device_ids=true, to_apply=%region_12.13 | all-reduce | flops 1 | bytes 8 | tf_op jit(solution)/shard_map/psum | solution.py:51
  109.6 3.1 %psum.29 = f32[]{:T(128)} all-reduce(f32[]{:T(128)} %psum.28), channel_id=1, replica_groups=mesh['img_0'=8,'img_1'=2,'txt_0'=4,'txt_1'=4] {'img_1'}, use_global_device_ids=true, to_apply=%region_13.14 | all-reduce | flops 1 | bytes 8 | tf_op jit(solution)/shard_map/psum | solution.py:51
  112.7 11.5 %psum.30 = f32[]{:T(128)} all-reduce(f32[]{:T(128)} %psum.29), channel_id=1, replica_groups=mesh['img_0'=8,'img_1'=2,'txt_0'=4,'txt_1'=4] {'txt_0'}, use_global_device_ids=true, to_apply=%region_14.15 | all-reduce | flops 1 | bytes 8 | tf_op jit(solution)/shard_map/psum | solution.py:51
  124.2 10.9 %psum.31 = f32[]{:T(128)} all-reduce(f32[]{:T(128)} %psum.30), channel_id=1, replica_groups=mesh['img_0'=8,'img_1'=2,'txt_0'=4,'txt_1'=4] {'txt_1'}, use_global_device_ids=true, to_apply=%region_15.16 | all-reduce | flops 1 | bytes 8 | tf_op jit(solution)/shard_map/psum | solution.py:51
  135.8 2.4 %reduce_sum.89 = f32[64,512]{1,0:T(8,128)} reduce(f32[16,64,512]{2,1,0:T(8,128)} %all-to-all-done.2, f32[]{:T(128)} %constant.4.clone.1), dimensions={0}, to_apply=%region_16.17 | reduce | flops 491520 | bytes 2228228 | tf_op jit(solution)/shard_map/reduce_sum | solution.py:73
  (81 shorter events, 1.6 us)
Async XLA Ops:
  7.2 1.7 %copy-start = (bf16[1024,1280]{1,0:T(8,128)(2,1)S(1)}, bf16[1024,1280]{1,0:T(8,128)(2,1)}, u32[]{:S(2)}) copy-start(bf16[1024,1280]{1,0:T(8,128)(2,1)} %param.4) | copy-start | bytes 7864324
  7.2 6.5 %copy-start.4 = (bf16[1024,512]{1,0:T(8,128)(2,1)S(1)}, bf16[1024,512]{1,0:T(8,128)(2,1)}, u32[]{:S(2)}) copy-start(bf16[1024,512]{1,0:T(8,128)(2,1)} %param.6) | copy-start | bytes 3145732
  8.9 4.8 %copy-start.6 = (bf16[1024,512]{1,0:T(8,128)(2,1)S(1)}, bf16[1024,512]{1,0:T(8,128)(2,1)}, u32[]{:S(2)}) copy-start(bf16[1024,512]{1,0:T(8,128)(2,1)} %param.7) | copy-start | bytes 3145732
  13.7 2.0 %copy-start.1 = (f32[1024,1024]{1,0:T(8,128)}, f32[1024,1024]{1,0:T(8,128)S(1)}, u32[]{:S(2)}) copy-start(f32[1024,1024]{1,0:T(8,128)S(1)} %get-tuple-element.50) | copy-start | bytes 12582916
  15.1 3.7 %copy-start.2 = (f32[1024,1024]{1,0:T(8,128)}, f32[1024,1024]{1,0:T(8,128)S(1)}, u32[]{:S(2)}) copy-start(f32[1024,1024]{1,0:T(8,128)S(1)} %get-tuple-element.49) | copy-start | bytes 12582916
  19.6 13.8 %all-to-all-start = ((f32[16,4,1024]{2,1,0:T(4,128)}), f32[16,4,1024]{2,1,0:T(4,128)S(1)}, u32[]{:S(2)}, u32[]{:S(2)}) async-start(f32[16,4,1024]{2,1,0:T(4,128)} %broadcast_in_dim.4), calls=%async_computation | async-start | bytes 524288 | tf_op jit(solution)/shard_map/all_to_all | solution.py:16
  34.2 19.8 %all-to-all-start.1 = ((f32[16,4,1024]{2,1,0:T(4,128)}), f32[16,4,1024]{2,1,0:T(4,128)S(1)}, u32[]{:S(2)}, u32[]{:S(2)}) async-start(f32[16,4,1024]{2,1,0:T(4,128)} %broadcast_in_dim.5), calls=%async_computation.1 | async-start | bytes 524288 | tf_op jit(solution)/shard_map/all_to_all | solution.py:16
  42.8 34.3 %reduce-scatter.3.cloned.1.call-start = ((), (), s32[]{:S(2)}) async-start(), calls=%async_computation.5 | async-start | bytes 3145728 | tf_op jit(solution)/shard_map/reduce_scatter | solution.py:66
  55.6 9.1 %copy-start.5 = (bf16[1024,512]{1,0:T(8,128)(2,1)S(1)}, bf16[1024,512]{1,0:T(8,128)(2,1)}, u32[]{:S(2)}) copy-start(bf16[1024,512]{1,0:T(8,128)(2,1)} %param.6) | copy-start | bytes 3145732
  64.7 2.9 %copy-start.3 = (bf16[1024,1024]{1,0:T(8,128)(2,1)}, bf16[1024,1024]{1,0:T(8,128)(2,1)S(1)}, u32[]{:S(2)}) copy-start(bf16[1024,1024]{1,0:T(8,128)(2,1)S(1)} %get-tuple-element.40) | copy-start | bytes 6291460
  67.6 70.6 %reduce-scatter.5.cloned.1.call-start = ((), (), s32[]{:S(2)}) async-start(), calls=%async_computation.6 | async-start | bytes 1179648 | tf_op jit(solution)/shard_map/reduce_scatter | solution.py:67
  81.6 54.2 %all-to-all-start.2 = ((f32[16,64,512]{2,1,0:T(8,128)}), f32[16,64,512]{2,1,0:T(8,128)}, u32[]{:S(2)}, u32[]{:S(2)}) async-start(f32[16,64,512]{2,1,0:T(8,128)} %bitcast.43), calls=%async_computation.2 | async-start | bytes 4194304 | tf_op jit(solution)/shard_map/all_to_all | solution.py:72
Sparse Core Ops, SparseCore 0:
  67.7 9.2 reduce-scatter.2
  80.3 39.9 reduce-scatter.4
where the time goes:
time: 147 us; the launch traced here: 146 us
  blocking collectives  43.5 us (30%)
  waiting for transfers between devices  27.8 us (19%)
  starting transfers between devices  21 us (14%)
  between operations  18.6 us (13%)
  other arithmetic  16.3 us (11%)
  matrix products  11.9 us (8%)
  local copies, waits for them, and re-layouts  7.03 us (5%)
    psum x4, blocking collectives, over_axes(): shard = lax.psum(shard, axis)  43.5 us
    all_to_all x2, waiting for transfers between devices, from_everyone(): return lax.all_to_all(copies, axis, split_axis=0, concat_axis=0, tiled=True)  18.3 us
    all_to_all x2, starting transfers between devices, from_everyone(): return lax.all_to_all(copies, axis, split_axis=0, concat_axis=0, tiled=True)  13.9 us
    reduce_scatter x1, waiting for transfers between devices, sum_by_chip(): parts = lax.psum_scatter(parts, core, scatter_dimension=0, tiled=True)  9.41 us
    reduce_sum x1, other arithmetic, body(): jnp.sum(p_col * gap) + jnp.sum(col_learn - col_teach) / img_count  9.09 us
    all_to_all x1, starting transfers between devices, summed_on_arrival(): parts = lax.all_to_all(split_up(shard, dim, size), axis, 0, 0, tiled=True)  6.9 us
    dot_general x1, matrix products, body(): jnp.einsum('id,jd->ij', teacher_img, teacher_txt, preferred_element_type=...  4.81 us
    dot_general x1, matrix products, body(): jnp.dot(picked, student_txt, preferred_element_type=jnp.float32)  4.46 us
  transfers between devices with their start and end apart: 5, of which 3 were waited for; matrix products, arithmetic and copies ran while one was open for 6% of the time, Pallas kernels for 0%

commit v1 on v0

--- a/solution.py
+++ b/solution.py
@@ -48,7 +48,7 @@
 
 def over_axes(shard, axes):
     for axis in axes:
-        shard = lax.psum(shard, axis)
+        shard = jnp.sum(lax.all_gather(shard, axis), axis=0)
     return shard
 
 

time: 147 us -> 154 us (1.048)
  local copies, waits for them, and re-layouts: 7.03 us -> 14.4 us
  other arithmetic: 16.3 us -> 18.7 us
  blocking collectives: 43.5 us -> 41.1 us
    psum x4 -> x0, blocking collectives: 43.5 us -> none  [over_axes(): shard = lax.psum(shard, axis)]
    unnamed x0 -> x4, blocking collectives: none -> 41.1 us
    unnamed x15 -> x35, local copies, waits for them, and re-layouts: 2.36 us -> 9.69 us
    reduce_sum x0 -> x4, other arithmetic: none -> 2.41 us  [over_axes(): shard = jnp.sum(lax.all_gather(shard, axis), axis=0)]
  transfers between devices with their start and end apart: 5 -> 5, of which waited for: 3 -> 3; matrix products, arithmetic and copies ran while one was open for 6% -> 12% of each run, Pallas kernels for 0% -> 0%
where the time goes in v1:
time: 154 us
  blocking collectives  41.1 us (27%)
  waiting for transfers between devices  27.8 us (18%)
  starting transfers between devices  21.2 us (14%)
  other arithmetic  18.7 us (12%)
  between operations  18.6 us (12%)
  local copies, waits for them, and re-layouts  14.4 us (9%)
  matrix products  11.9 us (8%)
    unnamed x4, blocking collectives  41.1 us
    all_to_all x2, waiting for transfers between devices, from_everyone(): return lax.all_to_all(copies, axis, split_axis=0, concat_axis=0, tiled=True)  18.3 us
    all_to_all x2, starting transfers between devices, from_everyone(): return lax.all_to_all(copies, axis, split_axis=0, concat_axis=0, tiled=True)  13.9 us
    unnamed x35, local copies, waits for them, and re-layouts  9.69 us
    reduce_scatter x1, waiting for transfers between devices, sum_by_chip(): parts = lax.psum_scatter(parts, core, scatter_dimension=0, tiled=True)  9.41 us
    reduce_sum x1, other arithmetic, body(): jnp.sum(p_col * gap) + jnp.sum(col_learn - col_teach) / img_count  9.09 us
    all_to_all x1, starting transfers between devices, summed_on_arrival(): parts = lax.all_to_all(split_up(shard, dim, size), axis, 0, 0, tiled=True)  7.04 us
    dot_general x1, matrix products, body(): jnp.einsum('id,jd->ij', teacher_img, teacher_txt, preferred_element_type=...  4.81 us
  transfers between devices with their start and end apart: 5, of which 3 were waited for; matrix products, arithmetic and copies ran while one was open for 12% of the time, Pallas kernels for 0%

profile of v1, /device:TPU:0, one launch (start us, length us, event | category | flops | bytes accessed | tf_op | source)
XLA Modules:
  0.0 153.7 jit_solution(4704066160310405661)
XLA Ops:
  7.2 1.7 %copy-done = bf16[1024,1280]{1,0:T(8,128)(2,1)S(1)} copy-done((bf16[1024,1280]{1,0:T(8,128)(2,1)S(1)}, bf16[1024,1280]{1,0:T(8,128)(2,1)}, u32[]{:S(2)}) %copy-start) | copy-done | bytes 2621464
  8.9 4.8 %multiply_reduce_fusion.4 = (f32[1024]{0:T(1024)S(1)}, f32[1024]{0:T(1024)S(1)}, f32[1024,1024]{1,0:T(8,128)S(1)}) fusion(bf16[1024,1280]{1,0:T(8,128)(2,1)S(1)} %copy-done, bf16[1024,1280]{1,0:T(8,128)(2,1)} %param.5), kind=kOutput, calls=%fused_computation.12 | convolution fusion | flops 2687498240 | bytes 9445376 | tf_op jit(solution)/shard_map/id,jd->ij/dot_general | solution.py:105
  13.7 1.4 multiply_reduce_fusion.2
  15.7 1.6 %exponential_reduce_fusion.1 = (f32[1024]{0:T(1024)S(1)}, f32[1024]{0:T(1024)S(1)}) fusion(f32[1024,1024]{1,0:T(8,128)S(1)} %get-tuple-element.50, f32[1024]{0:T(1024)S(1)} %get-tuple-element.7, f32[1024]{0:T(1024)S(1)} %get-tuple-element.8), kind=kLoop, calls=%fused_computation.4 | loop fusion | flops 5240832 | bytes 4210688 | tf_op jit(solution)/shard_map/reduce_sum | solution.py:93
  17.3 1.6 %exponential_reduce_fusion = (f32[1024]{0:T(1024)S(1)}, f32[1024]{0:T(1024)S(1)}) fusion(f32[1024,1024]{1,0:T(8,128)S(1)} %get-tuple-element.49, f32[1024]{0:T(1024)S(1)} %get-tuple-element.11, f32[1024]{0:T(1024)S(1)} %get-tuple-element.12), kind=kLoop, calls=%fused_computation.3 | loop fusion | flops 5240832 | bytes 4210688 | tf_op jit(solution)/shard_map/reduce_sum | solution.py:94
  18.9 0.8 broadcast_in_dim.4
  19.6 5.3 %all-to-all-start = ((f32[16,4,1024]{2,1,0:T(4,128)}), f32[16,4,1024]{2,1,0:T(4,128)S(1)}, u32[]{:S(2)}, u32[]{:S(2)}) async-start(f32[16,4,1024]{2,1,0:T(4,128)} %broadcast_in_dim.4), calls=%async_computation | async-start | bytes 524288 | tf_op jit(solution)/shard_map/all_to_all | solution.py:16
  25.0 8.5 %all-to-all-done = f32[16,4,1024]{2,1,0:T(4,128)S(1)} async-done(((f32[16,4,1024]{2,1,0:T(4,128)}), f32[16,4,1024]{2,1,0:T(4,128)S(1)}, u32[]{:S(2)}, u32[]{:S(2)}) %all-to-all-start) | async-done | bytes 262176 | tf_op jit(solution)/shard_map/all_to_all | solution.py:16
  33.4 0.8 broadcast_in_dim.5
  34.2 8.6 %all-to-all-start.1 = ((f32[16,4,1024]{2,1,0:T(4,128)}), f32[16,4,1024]{2,1,0:T(4,128)S(1)}, u32[]{:S(2)}, u32[]{:S(2)}) async-start(f32[16,4,1024]{2,1,0:T(4,128)} %broadcast_in_dim.5), calls=%async_computation.1 | async-start | bytes 524288 | tf_op jit(solution)/shard_map/all_to_all | solution.py:16
  44.1 9.9 %all-to-all-done.1 = f32[16,4,1024]{2,1,0:T(4,128)S(1)} async-done(((f32[16,4,1024]{2,1,0:T(4,128)}), f32[16,4,1024]{2,1,0:T(4,128)S(1)}, u32[]{:S(2)}, u32[]{:S(2)}) %all-to-all-start.1) | async-done | bytes 262176 | tf_op jit(solution)/shard_map/all_to_all | solution.py:16
  55.0 0.7 subtract_reduce_fusion
  55.6 9.1 %multiply_reduce_fusion = (f32[]{:T(128)}, f32[]{:T(128)}, bf16[1024,1024]{1,0:T(8,128)(2,1)S(1)}) fusion(f32[1024,1024]{1,0:T(8,128)} %copy-done.2, f32[1024,1024]{1,0:T(8,128)} %copy-done.1, f32[1024]{0:T(1024)S(1)} %bitcast.58, f32[1024]{0:T(1024)S(1)} %bitcast.55, f32[1024]{0:T(1024)S(1)} %bitcast.57, f32[1024]{0:T(1024)S(1)} %bitcast.53), kind=kLoop, calls=%fused_computation.1 | loop fusion | flops 16777214 | bytes 10502152 | tf_op jit(solution)/shard_map/reduce_sum | solution.py:129
  64.7 1.3 convolution_multiply_fusion
  66.0 1.6 %copy.21 = f32[2,8,64,512]{3,2,1,0:T(8,128)} copy(f32[2,8,64,512]{3,2,0,1:T(8,128)S(1)} %bitcast.52) | data formatting | bytes 4194304 | tf_op jit(solution)/shard_map/transpose | solution.py:65
  67.7 9.4 %reduce-scatter.3.cloned.1.call-done = f32[8,64,512]{2,1,0:T(8,128)} async-done(((f32[16,64,512]{2,1,0:T(8,128)}), f32[8,64,512]{2,1,0:T(8,128)}) %reduce-scatter.3.cloned.1.call-update) | async-done | bytes 1048592 | tf_op jit(solution)/shard_map/reduce_scatter | solution.py:66
  77.1 4.5 %convolution_multiply_fusion.1 = f32[1024,512]{1,0:T(8,128)} fusion(bf16[1024,1024]{1,0:T(8,128)(2,1)} %copy-done.3, bf16[1024,512]{1,0:T(8,128)(2,1)} %param.7), kind=kOutput, calls=%fused_computation.15 | convolution fusion | flops 1074266112 | bytes 5242880 | tf_op jit(solution)/shard_map/dot_general | solution.py:144
  81.6 7.0 %all-to-all-start.2 = ((f32[16,64,512]{2,1,0:T(8,128)}), f32[16,64,512]{2,1,0:T(8,128)}, u32[]{:S(2)}, u32[]{:S(2)}) async-start(f32[16,64,512]{2,1,0:T(8,128)} %bitcast.51), calls=%async_computation.2 | async-start | bytes 4194304 | tf_op jit(solution)/shard_map/all_to_all | solution.py:72
  88.6 0.6 dynamic-slice
  89.2 0.7 subtract_reduce_fusion.1
  92.4 0.7 dynamic-update-slice
  93.8 17.5 %all-reduce = f32[8]{0:T(128)S(1)} all-reduce(f32[8]{0:T(128)S(1)} %dynamic-update-slice), channel_id=1, replica_groups=mesh['img_0'=8,'img_1'=2,'txt_0'=4,'txt_1'=4] {'img_0'}, use_global_device_ids=true, to_apply=%add | all-reduce | flops 8 | bytes 64
  111.3 0.6 reduce_sum.125
  111.9 1.4 dynamic-update-slice.1
  113.9 2.4 %all-reduce.1 = f32[2]{0:T(128)S(1)} all-reduce(f32[2]{0:T(128)S(1)} %dynamic-update-slice.1), channel_id=1, replica_groups=mesh['img_0'=8,'img_1'=2,'txt_0'=4,'txt_1'=4] {'img_1'}, use_global_device_ids=true, to_apply=%add.1 | all-reduce | flops 2 | bytes 16
  116.3 0.6 reduce_sum.126
  116.9 1.4 dynamic-update-slice.2
  118.9 10.7 %all-reduce.2 = f32[4]{0:T(128)S(1)} all-reduce(f32[4]{0:T(128)S(1)} %dynamic-update-slice.2), channel_id=1, replica_groups=mesh['img_0'=8,'img_1'=2,'txt_0'=4,'txt_1'=4] {'txt_0'}, use_global_device_ids=true, to_apply=%add.2 | all-reduce | flops 4 | bytes 32
  129.7 0.6 reduce_sum.127
  130.3 1.4 dynamic-update-slice.3
  131.7 10.4 %all-reduce.3 = f32[4]{0:T(128)S(1)} all-reduce(f32[4]{0:T(128)S(1)} %dynamic-update-slice.3), channel_id=1, replica_groups=mesh['img_0'=8,'img_1'=2,'txt_0'=4,'txt_1'=4] {'txt_1'}, use_global_device_ids=true, to_apply=%add.3 | all-reduce | flops 4 | bytes 32
  143.3 2.4 %reduce_sum.129 = f32[64,512]{1,0:T(8,128)} reduce(f32[16,64,512]{2,1,0:T(8,128)} %all-to-all-done.2, f32[]{:T(128)} %constant.4.clone.1), dimensions={0}, to_apply=%region_16.17 | reduce | flops 491520 | bytes 2228228 | tf_op jit(solution)/shard_map/reduce_sum | solution.py:73
  (105 shorter events, 5.3 us)
Async XLA Ops:
  7.2 1.7 %copy-start = (bf16[1024,1280]{1,0:T(8,128)(2,1)S(1)}, bf16[1024,1280]{1,0:T(8,128)(2,1)}, u32[]{:S(2)}) copy-start(bf16[1024,1280]{1,0:T(8,128)(2,1)} %param.4) | copy-start | bytes 7864324
  7.2 6.5 %copy-start.4 = (bf16[1024,512]{1,0:T(8,128)(2,1)S(1)}, bf16[1024,512]{1,0:T(8,128)(2,1)}, u32[]{:S(2)}) copy-start(bf16[1024,512]{1,0:T(8,128)(2,1)} %param.6) | copy-start | bytes 3145732
  8.9 4.8 %copy-start.6 = (bf16[1024,512]{1,0:T(8,128)(2,1)S(1)}, bf16[1024,512]{1,0:T(8,128)(2,1)}, u32[]{:S(2)}) copy-start(bf16[1024,512]{1,0:T(8,128)(2,1)} %param.7) | copy-start | bytes 3145732
  13.7 2.0 %copy-start.1 = (f32[1024,1024]{1,0:T(8,128)}, f32[1024,1024]{1,0:T(8,128)S(1)}, u32[]{:S(2)}) copy-start(f32[1024,1024]{1,0:T(8,128)S(1)} %get-tuple-element.50) | copy-start | bytes 12582916
  15.1 3.7 %copy-start.2 = (f32[1024,1024]{1,0:T(8,128)}, f32[1024,1024]{1,0:T(8,128)S(1)}, u32[]{:S(2)}) copy-start(f32[1024,1024]{1,0:T(8,128)S(1)} %get-tuple-element.49) | copy-start | bytes 12582916
  19.6 13.8 %all-to-all-start = ((f32[16,4,1024]{2,1,0:T(4,128)}), f32[16,4,1024]{2,1,0:T(4,128)S(1)}, u32[]{:S(2)}, u32[]{:S(2)}) async-start(f32[16,4,1024]{2,1,0:T(4,128)} %broadcast_in_dim.4), calls=%async_computation | async-start | bytes 524288 | tf_op jit(solution)/shard_map/all_to_all | solution.py:16
  34.2 19.8 %all-to-all-start.1 = ((f32[16,4,1024]{2,1,0:T(4,128)}), f32[16,4,1024]{2,1,0:T(4,128)S(1)}, u32[]{:S(2)}, u32[]{:S(2)}) async-start(f32[16,4,1024]{2,1,0:T(4,128)} %broadcast_in_dim.5), calls=%async_computation.1 | async-start | bytes 524288 | tf_op jit(solution)/shard_map/all_to_all | solution.py:16
  42.8 34.3 %reduce-scatter.3.cloned.1.call-start = ((), (), s32[]{:S(2)}) async-start(), calls=%async_computation.5 | async-start | bytes 3145728 | tf_op jit(solution)/shard_map/reduce_scatter | solution.py:66
  55.6 9.1 %copy-start.5 = (bf16[1024,512]{1,0:T(8,128)(2,1)S(1)}, bf16[1024,512]{1,0:T(8,128)(2,1)}, u32[]{:S(2)}) copy-start(bf16[1024,512]{1,0:T(8,128)(2,1)} %param.6) | copy-start | bytes 3145732
  64.7 2.9 %copy-start.3 = (bf16[1024,1024]{1,0:T(8,128)(2,1)}, bf16[1024,1024]{1,0:T(8,128)(2,1)S(1)}, u32[]{:S(2)}) copy-start(bf16[1024,1024]{1,0:T(8,128)(2,1)S(1)} %get-tuple-element.40) | copy-start | bytes 6291460
  67.6 78.1 %reduce-scatter.5.cloned.1.call-start = ((), (), s32[]{:S(2)}) async-start(), calls=%async_computation.6 | async-start | bytes 1179648 | tf_op jit(solution)/shard_map/reduce_scatter | solution.py:67
  81.6 7.1 %copy-start.10 = (u32[256]{0:T(256)S(1)}, u32[256]{0:T(256)}, u32[]{:S(2)}) copy-start(u32[256]{0:T(256)} %constant.24) | copy-start | bytes 3076
  81.6 11.6 %copy-start.9 = (u32[256]{0:T(256)S(1)}, u32[256]{0:T(256)}, u32[]{:S(2)}) copy-start(u32[256]{0:T(256)} %constant.29) | copy-start | bytes 3076
  81.6 31.8 %copy-start.8 = (u32[256]{0:T(256)S(1)}, u32[256]{0:T(256)}, u32[]{:S(2)}) copy-start(u32[256]{0:T(256)} %constant.34) | copy-start | bytes 3076
  81.6 36.8 %copy-start.7 = (u32[256]{0:T(256)S(1)}, u32[256]{0:T(256)}, u32[]{:S(2)}) copy-start(u32[256]{0:T(256)} %constant.39) | copy-start | bytes 3076
  81.6 61.7 %all-to-all-start.2 = ((f32[16,64,512]{2,1,0:T(8,128)}), f32[16,64,512]{2,1,0:T(8,128)}, u32[]{:S(2)}, u32[]{:S(2)}) async-start(f32[16,64,512]{2,1,0:T(8,128)} %bitcast.51), calls=%async_computation.2 | async-start | bytes 4194304 | tf_op jit(solution)/shard_map/all_to_all | solution.py:72
Sparse Core Ops, SparseCore 0:
  67.7 9.2 reduce-scatter.2
  80.3 40.1 reduce-scatter.4
